TPU v7x, 32 devices: a whole 2x2x4 slice. The times are simulated.
32 devices in a mesh: wide: 8 (over z, y), narrow: 4 (over x, core).
Axes of the slice: x: 2, y: 2, z: 4, core: 2. Of those that a mesh axis runs over, the one named last changes fastest.
Arguments:
- media_feats: bfloat16 [8, 2048, 1536], P('wide', 'narrow'), may hold values from -6 to 6
- latents: bfloat16 [8, 64, 1536], P('wide', 'narrow'), may hold values from -6 to 6
- frame_counts: int32 [8], P('wide'), may hold values from 1 to 8, as said below
- media_mask: int32 [8, 2048], P('wide'), may hold values 0 or 1
- time_embed: bfloat16 [8, 1536], replicated, may hold values from -3 to 3
- media_gain: float32 [1536], replicated, may hold values from 0.1 to 1.9
- media_bias: float32 [1536], replicated, may hold values from -1.75 to 1.75
- latent_gain: float32 [1536], replicated, may hold values from 0.1 to 1.9
- latent_bias: float32 [1536], replicated, may hold values from -1.75 to 1.75
- ffn_gain: float32 [1536], replicated, may hold values from 0.1 to 1.9
- ffn_bias: float32 [1536], replicated, may hold values from -1.75 to 1.75
- query_weight: bfloat16 [1536, 1536], P('wide', 'narrow'), may hold values from -0.3125 to 0.3125
- keyval_weight: bfloat16 [1536, 2, 1536], P('wide', None, 'narrow'), may hold values from -0.15625 to 0.15625
- output_weight: bfloat16 [1536, 1536], P('narrow', 'wide'), may hold values from -0.625 to 0.625
- up_weight: bfloat16 [1536, 6144], P(None, 'narrow'), may hold values from -0.15625 to 0.15625
- down_weight: bfloat16 [6144, 1536], P('narrow'), may hold values from -0.078125 to 0.078125
- cotangent: bfloat16 [8, 64, 1536], P('wide', 'narrow'), may hold values from -6 to 6
Outputs:
- out_latents: bfloat16 [8, 64, 1536], P('wide', 'narrow')
- grad_media: bfloat16 [8, 2048, 1536], P('wide', 'narrow')
- grad_latents: bfloat16 [8, 64, 1536], P('wide', 'narrow')
- grad_time_embed: float32 [8, 1536], P(None, ('wide', 'narrow'))
- grad_media_gain: float32 [1536], P(('wide', 'narrow'))
- grad_media_bias: float32 [1536], P(('wide', 'narrow'))
- grad_latent_gain: float32 [1536], P(('wide', 'narrow'))
- grad_latent_bias: float32 [1536], P(('wide', 'narrow'))
- grad_ffn_gain: float32 [1536], P(('wide', 'narrow'))
- grad_ffn_bias: float32 [1536], P(('wide', 'narrow'))
- grad_query_weight: float32 [1536, 1536], P('wide', 'narrow')
- grad_keyval_weight: float32 [1536, 2, 1536], P('wide', None, 'narrow')
- grad_output_weight: float32 [1536, 1536], P('narrow', 'wide')
- grad_up_weight: float32 [1536, 6144], P('wide', 'narrow')
- grad_down_weight: float32 [6144, 1536], P('narrow', 'wide')
Inputs may be any that keep to these rules, and one draw needn't show every extreme that they name: `frame_counts`: frames of each item; some item has exactly 8.
All inputs are finite; a program needn't handle non-finite values. No bound on the sum of `media_mask` on one device may be relied on, other than what follows from the above.
Results may differ from a plain program's by a relative error of at most 0.02.
Values may be sent and summed in bfloat16 or wider, within the bound.
A program may use at most 128 MiB of HBM per device.

v0:
```python
import math
import jax
import jax.numpy as jnp
from jax import lax
from jax.sharding import PartitionSpec as P

HEADS = 16
HEAD_DIM = 96
FRAMES_MAX = 8
PATCHES = 256
EPS = 1e-05
ENT_COEF = 4.0
HIGH = lax.Precision.HIGHEST


def norm_forward(values, norm_gain, norm_bias):
    row_mean = jnp.mean(values, axis=-1, keepdims=True)
    centered = values - row_mean
    inv_std = lax.rsqrt(jnp.mean(centered * centered, axis=-1, keepdims=True) + EPS)
    normed = centered * inv_std
    return (normed * norm_gain + norm_bias, normed, inv_std)


def norm_backward(grad_out, normed, inv_std, norm_gain):
    scaled = grad_out * norm_gain
    grad_in = inv_std * (
        scaled
        - jnp.mean(scaled, axis=-1, keepdims=True)
        - normed * jnp.mean(scaled * normed, axis=-1, keepdims=True)
    )
    return (grad_in, jnp.sum(grad_out * normed, axis=0), jnp.sum(grad_out, axis=0))


def gelu_slope(pre_act):
    cdf_part = 0.5 * (1.0 + lax.erf(pre_act * (1.0 / math.sqrt(2.0))))
    density = jnp.exp(-0.5 * pre_act * pre_act) * (1.0 / math.sqrt(2.0 * math.pi))
    return cdf_part + pre_act * density


def body(
    media_feats,
    latents,
    frame_counts,
    media_mask,
    time_embed,
    media_gain,
    media_bias,
    latent_gain,
    latent_bias,
    ffn_gain,
    ffn_bias,
    query_weight,
    keyval_weight,
    output_weight,
    up_weight,
    down_weight,
    cotangent,
):
    item_count = media_feats.shape[0]
    own_media = media_feats.shape[1]
    width = media_feats.shape[2]
    own_latent = latents.shape[1]
    narrow_size = lax.axis_size("narrow")
    narrow_pos = lax.axis_index("narrow")
    media_total = own_media * narrow_size
    latent_total = own_latent * narrow_size
    head_local = HEADS // narrow_size
    cols = head_local * HEAD_DIM
    key_total = media_total + latent_total
    all_ids = jnp.arange(media_total, dtype=jnp.int32) // PATCHES
    valid_tok = (all_ids[None, :] < frame_counts[:, None]) & (media_mask > 0)
    local_count = jnp.sum(valid_tok.astype(jnp.float32)) + float(item_count * latent_total)
    total_count = lax.psum(local_count, "wide")
    all_items = item_count * lax.axis_size("wide")
    ent_weight = ENT_COEF * float(all_items * media_total) / total_count
    query_own, keyval_own, output_own = (
        lax.all_gather(query_weight, "wide", axis=0, tiled=True),
        lax.all_gather(keyval_weight, "wide", axis=0, tiled=True),
        lax.all_gather(output_weight, "wide", axis=1, tiled=True),
    )
    query_full, keyval_full = (
        lax.all_gather(query_own, "narrow", axis=1, tiled=True),
        lax.all_gather(keyval_own, "narrow", axis=2, tiled=True),
    )
    keyval_flat = keyval_own.reshape(width, 2 * cols)
    own_ids = (narrow_pos * own_media + jnp.arange(own_media, dtype=jnp.int32)) // PATCHES
    frame_onehot = own_ids[:, None] == jnp.arange(FRAMES_MAX, dtype=jnp.int32)[None, :]
    time_rows = jnp.dot(
        frame_onehot.astype(jnp.bfloat16), time_embed, preferred_element_type=jnp.float32
    )
    score_scale = HEAD_DIM ** (-0.5)

    def item_step(carry, item):
        (
            down_acc,
            up_acc,
            output_acc,
            keyval_acc,
            query_acc,
            mg_acc,
            mb_acc,
            lg_acc,
            lb_acc,
            fg_acc,
            fb_acc,
            time_acc,
        ) = carry
        media_one, latent_one, valid_one, cot_one = item
        media_nf, media_hat, media_istd = norm_forward(
            media_one.astype(jnp.float32) + time_rows, media_gain, media_bias
        )
        latent_f32 = latent_one.astype(jnp.float32)
        latent_nf, latent_hat, latent_istd = norm_forward(latent_f32, latent_gain, latent_bias)
        media_all, latent_all = (
            lax.all_gather(media_nf.astype(jnp.bfloat16), "narrow", axis=0, tiled=True),
            lax.all_gather(latent_nf.astype(jnp.bfloat16), "narrow", axis=0, tiled=True),
        )
        keys_in = jnp.concatenate([media_all, latent_all], axis=0)
        query_act = jnp.dot(latent_all, query_own, preferred_element_type=jnp.float32).astype(
            jnp.bfloat16
        )
        key_vals = jnp.dot(keys_in, keyval_flat, preferred_element_type=jnp.float32).astype(
            jnp.bfloat16
        )
        query_heads = query_act.reshape(latent_total, head_local, HEAD_DIM)
        key_heads = key_vals[:, :cols].reshape(key_total, head_local, HEAD_DIM)
        value_heads = key_vals[:, cols:].reshape(key_total, head_local, HEAD_DIM)
        key_valid = jnp.concatenate([valid_one, jnp.ones((latent_total,), dtype=bool)])
        scores = (
            jnp.einsum("lhd,khd->hlk", query_heads, key_heads, preferred_element_type=jnp.float32)
            * score_scale
        )
        open_keys = key_valid[None, None, :]
        masked = jnp.where(open_keys, scores, -1e30)
        row_top = jnp.max(masked, axis=-1)
        expo = jnp.exp(masked - row_top[..., None])
        prob_all = expo / jnp.sum(expo, axis=-1)[..., None]
        prob_low = prob_all.astype(jnp.bfloat16)
        plain_scores = jnp.where(open_keys, scores, 0.0)
        mean_score = jnp.sum(prob_all * plain_scores, axis=-1)
        attn_out = jnp.einsum(
            "hlk,khd->lhd", prob_low, value_heads, preferred_element_type=jnp.float32
        ).reshape(latent_total, cols)
        attn_low = attn_out.astype(jnp.bfloat16)
        branch_part = jnp.dot(attn_low, output_own, preferred_element_type=jnp.float32)
        branch_own = lax.psum_scatter(
            branch_part.astype(jnp.bfloat16), "narrow", scatter_dimension=0, tiled=True
        ).astype(jnp.float32)
        latent_mid = latent_f32 + branch_own
        hidden_f, hidden_hat, hidden_istd = norm_forward(latent_mid, ffn_gain, ffn_bias)
        hidden_all, cot_all = (
            lax.all_gather(hidden_f.astype(jnp.bfloat16), "narrow", axis=0, tiled=True),
            lax.all_gather(cot_one, "narrow", axis=0, tiled=True),
        )
        pre_act = jnp.dot(hidden_all, up_weight, preferred_element_type=jnp.float32)
        act_low = jax.nn.gelu(pre_act, approximate=False).astype(jnp.bfloat16)
        ffn_part = jnp.dot(act_low, down_weight, preferred_element_type=jnp.float32)
        ffn_own = lax.psum_scatter(
            ffn_part.astype(jnp.bfloat16), "narrow", scatter_dimension=0, tiled=True
        ).astype(jnp.float32)
        out_one = (latent_mid + ffn_own).astype(jnp.bfloat16)
        down_acc = down_acc + jnp.einsum(
            "lf,ld->fd", act_low, cot_all, preferred_element_type=jnp.float32
        )
        grad_act = jnp.einsum("ld,fd->lf", cot_all, down_weight, preferred_element_type=jnp.float32)
        grad_pre = (grad_act * gelu_slope(pre_act)).astype(jnp.bfloat16)
        up_acc = up_acc + jnp.einsum(
            "ld,lf->df", hidden_all, grad_pre, preferred_element_type=jnp.float32
        )
        hidden_part = jnp.einsum(
            "lf,df->ld", grad_pre, up_weight, preferred_element_type=jnp.float32
        )
        grad_hidden = lax.psum_scatter(
            hidden_part.astype(jnp.bfloat16), "narrow", scatter_dimension=0, tiled=True
        ).astype(jnp.float32)
        grad_norm, fg_part, fb_part = norm_backward(grad_hidden, hidden_hat, hidden_istd, ffn_gain)
        grad_mid = cot_one.astype(jnp.float32) + grad_norm
        grad_branch_all = lax.all_gather(
            grad_mid.astype(jnp.bfloat16), "narrow", axis=0, tiled=True
        )
        output_acc = output_acc + jnp.einsum(
            "lc,ld->cd", attn_low, grad_branch_all, preferred_element_type=jnp.float32
        )
        grad_attn = jnp.einsum(
            "ld,cd->lc", grad_branch_all, output_own, preferred_element_type=jnp.float32
        ).astype(jnp.bfloat16)
        row_dots = jnp.sum(
            (grad_attn.astype(jnp.float32) * attn_out).reshape(latent_total, head_local, HEAD_DIM),
            axis=-1,
        )
        shift_rows = (jnp.transpose(row_dots, (1, 0)) - ent_weight * mean_score)[..., None]
        grad_heads = grad_attn.reshape(latent_total, head_local, HEAD_DIM)
        grad_prob = jnp.einsum(
            "lhd,khd->hlk", grad_heads, value_heads, preferred_element_type=jnp.float32
        )
        grad_scores = (prob_all * (grad_prob - ent_weight * plain_scores - shift_rows)).astype(
            jnp.bfloat16
        )
        grad_values = jnp.einsum(
            "hlk,lhd->khd", prob_low, grad_heads, preferred_element_type=jnp.float32
        ).reshape(key_total, cols)
        grad_keys = (
            jnp.einsum(
                "hlk,lhd->khd", grad_scores, query_heads, preferred_element_type=jnp.float32
            ).reshape(key_total, cols)
            * score_scale
        )
        grad_query = (
            jnp.einsum(
                "hlk,khd->lhd", grad_scores, key_heads, preferred_element_type=jnp.float32
            ).reshape(latent_total, cols)
            * score_scale
        ).astype(jnp.bfloat16)
        grad_pairs = jnp.concatenate([grad_keys, grad_values], axis=-1).astype(jnp.bfloat16)
        keyval_acc = keyval_acc + jnp.einsum(
            "kd,ke->de", keys_in, grad_pairs, preferred_element_type=jnp.float32
        )
        query_acc = query_acc + jnp.einsum(
            "ld,lc->dc", latent_all, grad_query, preferred_element_type=jnp.float32
        )
        media_pairs = grad_pairs[:media_total].reshape(media_total, 2, cols)
        latent_pairs = jnp.concatenate(
            [
                grad_pairs[media_total:].reshape(latent_total, 2, cols),
                grad_query.reshape(latent_total, 1, cols),
            ],
            axis=1,
        )
        media_back, latent_back = (
            lax.all_to_all(media_pairs, "narrow", split_axis=0, concat_axis=2, tiled=True),
            lax.all_to_all(latent_pairs, "narrow", split_axis=0, concat_axis=2, tiled=True),
        )
        grad_media_rows = jnp.einsum(
            "rsc,dsc->rd", media_back, keyval_full, preferred_element_type=jnp.float32
        )
        grad_latent_normed = jnp.einsum(
            "rsc,dsc->rd", latent_back[:, :2], keyval_full, preferred_element_type=jnp.float32
        ) + jnp.einsum(
            "rc,dc->rd", latent_back[:, 2], query_full, preferred_element_type=jnp.float32
        )
        grad_media_in, mg_part, mb_part = norm_backward(
            grad_media_rows, media_hat, media_istd, media_gain
        )
        time_acc = time_acc + jnp.einsum(
            "mf,md->fd", frame_onehot.astype(jnp.float32), grad_media_in, precision=HIGH
        )
        grad_latent_in, lg_part, lb_part = norm_backward(
            grad_latent_normed, latent_hat, latent_istd, latent_gain
        )
        grad_latent_one = (grad_mid + grad_latent_in).astype(jnp.bfloat16)
        carry = (
            down_acc,
            up_acc,
            output_acc,
            keyval_acc,
            query_acc,
            mg_acc + mg_part,
            mb_acc + mb_part,
            lg_acc + lg_part,
            lb_acc + lb_part,
            fg_acc + fg_part,
            fb_acc + fb_part,
            time_acc,
        )
        return (carry, (out_one, grad_media_in.astype(jnp.bfloat16), grad_latent_one))

    ff_local = up_weight.shape[1]
    vector_zero = jnp.zeros((width,), jnp.float32)
    start = (
        jnp.zeros((ff_local, width), jnp.float32),
        jnp.zeros((width, ff_local), jnp.float32),
        jnp.zeros((cols, width), jnp.float32),
        jnp.zeros((width, 2 * cols), jnp.float32),
        jnp.zeros((width, cols), jnp.float32),
        vector_zero,
        vector_zero,
        vector_zero,
        vector_zero,
        vector_zero,
        vector_zero,
        jnp.zeros((FRAMES_MAX, width), jnp.float32),
    )
    totals, stacked = lax.scan(item_step, start, (media_feats, latents, valid_tok, cotangent))
    (
        down_acc,
        up_acc,
        output_acc,
        keyval_acc,
        query_acc,
        mg_acc,
        mb_acc,
        lg_acc,
        lb_acc,
        fg_acc,
        fb_acc,
        time_acc,
    ) = totals
    out_latents, grad_media, grad_latents = stacked
    up_sum, down_sum, query_sum, keyval_sum, output_sum = (
        lax.psum_scatter(
            up_acc.astype(jnp.bfloat16), "wide", scatter_dimension=0, tiled=True
        ).astype(jnp.float32),
        lax.psum_scatter(
            down_acc.astype(jnp.bfloat16), "wide", scatter_dimension=1, tiled=True
        ).astype(jnp.float32),
        lax.psum_scatter(
            query_acc.astype(jnp.bfloat16), "wide", scatter_dimension=0, tiled=True
        ).astype(jnp.float32),
        lax.psum_scatter(
            keyval_acc.reshape(width, 2, cols).astype(jnp.bfloat16),
            "wide",
            scatter_dimension=0,
            tiled=True,
        ).astype(jnp.float32),
        lax.psum_scatter(
            output_acc.astype(jnp.bfloat16), "wide", scatter_dimension=1, tiled=True
        ).astype(jnp.float32),
    )
    mg_sum, mb_sum, lg_sum, lb_sum, fg_sum, fb_sum, time_sum = (
        lax.psum_scatter(mg_acc, ("wide", "narrow"), scatter_dimension=0, tiled=True),
        lax.psum_scatter(mb_acc, ("wide", "narrow"), scatter_dimension=0, tiled=True),
        lax.psum_scatter(lg_acc, ("wide", "narrow"), scatter_dimension=0, tiled=True),
        lax.psum_scatter(lb_acc, ("wide", "narrow"), scatter_dimension=0, tiled=True),
        lax.psum_scatter(fg_acc, ("wide", "narrow"), scatter_dimension=0, tiled=True),
        lax.psum_scatter(fb_acc, ("wide", "narrow"), scatter_dimension=0, tiled=True),
        lax.psum_scatter(time_acc, ("wide", "narrow"), scatter_dimension=1, tiled=True),
    )
    return (
        out_latents,
        grad_media,
        grad_latents,
        time_sum,
        mg_sum,
        mb_sum,
        lg_sum,
        lb_sum,
        fg_sum,
        fb_sum,
        query_sum,
        keyval_sum,
        output_sum,
        up_sum,
        down_sum,
    )


def solution(mesh):
    placed = (
        P("wide", "narrow", None),
        P("wide", "narrow", None),
        P("wide"),
        P("wide", None),
        P(),
        P(),
        P(),
        P(),
        P(),
        P(),
        P(),
        P("wide", "narrow"),
        P("wide", None, "narrow"),
        P("narrow", "wide"),
        P(None, "narrow"),
        P("narrow", None),
        P("wide", "narrow", None),
    )
    return jax.shard_map(
        body,
        mesh=mesh,
        in_specs=placed,
        out_specs=(
            P("wide", "narrow", None),
            P("wide", "narrow", None),
            P("wide", "narrow", None),
            P(None, ("wide", "narrow")),
            P(("wide", "narrow")),
            P(("wide", "narrow")),
            P(("wide", "narrow")),
            P(("wide", "narrow")),
            P(("wide", "narrow")),
            P(("wide", "narrow")),
            P("wide", "narrow"),
            P("wide", None, "narrow"),
            P("narrow", "wide"),
            P("wide", "narrow"),
            P("narrow", "wide"),
        ),
        check_vma=False,
    )
```

profile of v0, /device:TPU:0, one launch (start us, length us, event | category | flops | bytes accessed | tf_op | source)
XLA Modules:
  0.0 941.4 jit_solution(12498868731809088327)
XLA Ops:
  15.3 6.9 all_gather.36
  23.6 30.5 %all-gather.12.cloned.1.call-done = bf16[1536,384]{1,0:T(8,128)(2,1)} async-done(((bf16[192,384]{1,0:T(8,128)(2,1)}), bf16[1536,384]{1,0:T(8,128)(2,1)}) %all-gather.12.cloned.1.call-update) | async-done | bytes 1179664 | tf_op jit(solution)/shard_map/all_gather | solution.py:77
  55.8 51.6 %all-gather.10.cloned.1.call-done = bf16[1536,2,384]{2,0,1:T(8,128)(2,1)} async-done(((bf16[192,2,384]{2,0,1:T(8,128)(2,1)}), bf16[1536,2,384]{2,0,1:T(8,128)(2,1)}) %all-gather.10.cloned.1.call-update) | async-done | bytes 2359312 | tf_op jit(solution)/shard_map/all_gather | solution.py:78
  107.4 4.3 copy.117
  111.7 42.8 %all-gather.8.cloned.1.call-done = bf16[2048,1536]{1,0:T(8,128)(2,1)} async-done(((bf16[512,1536]{1,0:T(8,128)(2,1)}), bf16[2048,1536]{1,0:T(8,128)(2,1)}) %all-gather.8.cloned.1.call-update) | async-done | bytes 6291472 | tf_op jit(solution)/shard_map/while/body/eval_jaxpr/all_gather | solution.py:115
  154.4 3.3 constant_dynamic-update-slice_fusion.1
  157.9 5.5 convolution_convert_fusion.2
  165.4 3.7 copy.119
  169.2 3.8 copy.118
  173.0 3.6 fusion.82
  176.6 3.0 convolution_bitcast_fusion.3
  181.3 16.3 %all-gather.14.cloned.1.call-done = bf16[384,1536]{0,1:T(8,128)(2,1)} async-done(((bf16[384,192]{0,1:T(8,128)(2,1)}), bf16[384,1536]{0,1:T(8,128)(2,1)}) %all-gather.14.cloned.1.call-update) | async-done | bytes 1179664 | tf_op jit(solution)/shard_map/all_gather | solution.py:79
  197.6 2.4 convolution_convert_fusion.9
  200.1 7.1 all-gather
  207.2 11.8 %reduce-scatter.11.cloned.1.call-done = bf16[16,1536]{1,0:T(8,128)(2,1)} async-done(((bf16[64,1536]{1,0:T(8,128)(2,1)}), bf16[16,1536]{1,0:T(8,128)(2,1)}) %reduce-scatter.11.cloned.1.call-update) | async-done | bytes 49168 | tf_op jit(solution)/shard_map/while/body/eval_jaxpr/reduce_scatter | solution.py:146
  221.9 5.6 all_gather.40
  228.2 3.3 fusion.85
  231.5 4.0 fusion.8
  236.2 4.6 convolution_convert_fusion.7
  241.6 19.1 %reduce-scatter.15.cloned.1.call-done = bf16[16,1536]{1,0:T(8,128)(2,1)} async-done(((bf16[64,1536]{1,0:T(8,128)(2,1)}), bf16[16,1536]{1,0:T(8,128)(2,1)}) %reduce-scatter.15.cloned.1.call-update) | async-done | bytes 49168 | tf_op jit(solution)/shard_map/while/body/eval_jaxpr/reduce_scatter | solution.py:173
  263.2 5.6 all_gather.42
  269.4 2.5 convolution_convert_fusion.5
  272.6 22.0 %psum.7 = f32[]{:T(128)} all-reduce(f32[]{:T(128)S(6)} %add.196), channel_id=1, replica_groups=mesh['wide'=8,'narrow'=4] {'wide'}, use_global_device_ids=true, to_apply=%region_14.15 | all-reduce | flops 1 | bytes 8 | tf_op jit(solution)/shard_map/psum | solution.py:73
  295.4 4.2 multiply_reduce_fusion.4
  304.1 3.6 fusion.6
  313.9 2.9 convolution_convert_fusion.3
  316.8 10.9 %convolution_convert_fusion.4 = bf16[1536,768]{0,1:T(8,128)(2,1)} fusion(bf16[2112,1536]{1,0:T(8,128)(2,1)} %copy-done.6, bf16[2112,384]{0,1:T(8,128)(2,1)S(1)} %bitcast.160, bf16[2112,384]{0,1:T(8,128)(2,1)S(1)} %bitcast.155), kind=kOutput, calls=%fused_computation.19 | convolution fusion | flops 4990500864 | bytes 12091392 | tf_op jit(solution)/shard_map/while/body/eval_jaxpr/kd,ke->de/dot_general | solution.py:215
  327.7 6.9 copy.135
  335.3 3.5 fusion.7
  338.8 8.7 copy.126
  347.6 4.7 all-to-all-start
  352.3 4.7 convolution_convert_fusion.8
  357.3 31.9 %all-to-all-done = bf16[2048,2,384]{2,1,0:T(2,128)(2,1)} async-done(((bf16[2048,2,384]{2,1,0:T(2,128)(2,1)}), bf16[2048,2,384]{2,1,0:T(2,128)(2,1)}, u32[]{:S(2)}, u32[]{:S(2)}) %all-to-all-start) | async-done | bytes 3145760 | tf_op jit(solution)/shard_map/while/body/eval_jaxpr/all_to_all | solution.py:230
  393.5 10.0 %multiply_reduce_fusion = (f32[1536]{0:T(1024)}, f32[512]{0:T(512)S(1)}, f32[512]{0:T(512)S(1)}, f32[1536]{0:T(1024)}, f32[512,1536]{1,0:T(8,128)S(1)}) fusion(f32[512,1536]{1,0:T(8,128)S(1)} %get-tuple-element.150, f32[512]{0:T(512)S(1)} %add_rsqrt_fusion, f32[512]{0:T(512)S(1)} %broadcast_multiply_fusion.2, f32[1536]{0:T(1024)S(1)} %copy-done.33, ...), kind=kOutput, calls=%fused_computation.23 | convolution fusion | flops 4838912000 | bytes 18900992 | tf_op jit(solution)/shard_map/while/body/eval_jaxpr/rsc,dsc->rd/dot_general | solution.py:233
  405.6 3.6 convolution_bitcast_fusion.1
  409.3 3.5 convolution_convert_fusion.1
  413.9 3.9 convolution_convert_fusion
  421.3 3.6 all-to-all-start.1
  426.2 3.8 all-to-all-done.1
  431.6 31.3 %reduce-scatter.17.cloned.1.call-done = bf16[192,384]{1,0:T(8,128)(2,1)} async-done(((bf16[1536,384]{1,0:T(8,128)(2,1)}), bf16[192,384]{1,0:T(8,128)(2,1)}) %reduce-scatter.17.cloned.1.call-update) | async-done | bytes 147472 | tf_op jit(solution)/shard_map/reduce_scatter | solution.py:306
  464.6 109.4 %all-reduce.11.cloned.1.call-done = bf16[1536,2,384]{2,1,0:T(2,128)(2,1)} async-done(((bf16[1536,2,384]{2,1,0:T(2,128)(2,1)}), bf16[1536,2,384]{2,1,0:T(2,128)(2,1)}) %all-reduce.11.cloned.1.call-update) | async-done | bytes 2359312
  576.0 6.2 convolution_bitcast_fusion.2
  582.3 29.8 %all-gather.18.cloned.1.call-done = bf16[1536,1536]{1,0:T(8,128)(2,1)} async-done(((bf16[1536,384]{1,0:T(8,128)(2,1)}), bf16[1536,1536]{1,0:T(8,128)(2,1)}) %all-gather.18.cloned.1.call-update) | async-done | bytes 4718608 | tf_op jit(solution)/shard_map/all_gather | solution.py:82
  612.1 3.8 fusion.53
  616.0 40.1 %all-reduce.8 = (f32[1536]{0:T(1024)S(1)}, f32[1536]{0:T(1024)S(1)}, f32[1536]{0:T(1024)S(1)}, f32[1536]{0:T(1024)S(1)}, f32[1536]{0:T(1024)S(1)}, /*index=5*/f32[1536]{0:T(1024)S(1)}) all-reduce(f32[1536]{0:T(1024)S(1)} %copy-done.46, f32[1536]{0:T(1024)S(1)} %copy-done.47, ...), channel_id=7, replica_groups=mesh['wide'=8,'narrow'=4] {'wide','narrow'}, use_global_device_ids=true, to_apply=%region_23.24.clone | all-reduce | flops 9216 | bytes 73728
  661.2 74.4 %reduce-scatter.25.cloned.1.call-done = f32[48,8]{1,0:T(8,128)} async-done(((f32[1536,8]{1,0:T(8,128)}), f32[48,8]{1,0:T(8,128)}) %reduce-scatter.25.cloned.1.call-update) | async-done | bytes 1552
  737.0 96.9 %reduce-scatter.21.cloned.1.call-done = bf16[192,1536]{1,0:T(8,128)(2,1)} async-done(((bf16[1536,1536]{1,0:T(8,128)(2,1)}), bf16[192,1536]{1,0:T(8,128)(2,1)}) %reduce-scatter.21.cloned.1.call-update) | async-done | bytes 589840 | tf_op jit(solution)/shard_map/reduce_scatter | solution.py:300
  836.0 96.6 %reduce-scatter.23.cloned.1.call-done = bf16[1536,192]{0,1:T(8,128)(2,1)} async-done(((bf16[1536,1536]{0,1:T(8,128)(2,1)}), bf16[1536,192]{0,1:T(8,128)(2,1)}) %reduce-scatter.23.cloned.1.call-update) | async-done | bytes 589840 | tf_op jit(solution)/shard_map/reduce_scatter | solution.py:303
  (218 shorter events, 61.9 us)
Async XLA Ops:
  7.2 46.9 %all-gather.12.cloned.1.call-start = ((), (), s32[]{:S(2)}) async-start(), calls=%async_computation.12 | async-start | bytes 1327104 | tf_op jit(solution)/shard_map/all_gather | solution.py:77
  7.9 99.4 %all-gather.10.cloned.1.call-start = ((), (), s32[]{:S(2)}) async-start(), calls=%async_computation.11 | async-start | bytes 2654208 | tf_op jit(solution)/shard_map/all_gather | solution.py:78
  9.7 144.7 %all-gather.8.cloned.1.call-start = ((), (), s32[]{:S(2)}) async-start(), calls=%async_computation.10 | async-start | bytes 7864320 | tf_op jit(solution)/shard_map/while/body/eval_jaxpr/all_gather | solution.py:115
  12.5 10.4 %copy-start.45 = (s32[1,2048]{1,0:T(1,128)S(1)}, s32[1,2048]{1,0:T(1,128)}, u32[]{:S(2)}) copy-start(s32[1,2048]{1,0:T(1,128)} %param.20) | copy-start | bytes 24580
  14.2 183.4 %all-gather.14.cloned.1.call-start = ((), (), s32[]{:S(2)}) async-start(), calls=%async_computation.13 | async-start | bytes 1327104 | tf_op jit(solution)/shard_map/all_gather | solution.py:79
  14.8 204.2 %reduce-scatter.11.cloned.1.call-start = ((), (), s32[]{:S(2)}) async-start(), calls=%async_computation.14 | async-start | bytes 245760 | tf_op jit(solution)/shard_map/while/body/eval_jaxpr/reduce_scatter | solution.py:146
  15.0 7.9 copy-start.39
  15.2 7.6 copy-start.48
  23.5 149.4 %copy-start.54 = (pred[2112]{0:T(1024)(128)(4,1)}, pred[2112]{0:T(1024)(128)(4,1)S(1)}, u32[]{:S(2)}) copy-start(pred[2112]{0:T(1024)(128)(4,1)S(1)} %concatenate.18) | copy-start | bytes 6340
  55.8 117.2 %copy-start.27 = (bf16[64,4,96]{2,1,0:T(4,128)(2,1)}, bf16[64,4,96]{2,1,0:T(4,128)(2,1)S(1)}, u32[]{:S(2)}) copy-start(bf16[64,4,96]{2,1,0:T(4,128)(2,1)S(1)} %reshape.235) | copy-start | bytes 147460
  176.6 127.5 %copy-start.57 = (f32[4,64]{1,0:T(4,128)}, f32[4,64]{1,0:T(4,128)S(1)}, u32[]{:S(2)}) copy-start(f32[4,64]{1,0:T(4,128)S(1)} %get-tuple-element.151) | copy-start | bytes 3076
  176.6 44.4 %copy-start.28 = (f32[1536]{0:T(1024)S(1)}, f32[1536]{0:T(1024)}, u32[]{:S(2)}) copy-start(f32[1536]{0:T(1024)} %param.26) | copy-start | bytes 18436
  176.6 44.4 %copy-start.44 = (f32[1536]{0:T(1024)S(1)}, f32[1536]{0:T(1024)}, u32[]{:S(2)}) copy-start(f32[1536]{0:T(1024)} %param.27) | copy-start | bytes 18436
  181.3 50.1 %copy-start.18 = (f32[64,384]{1,0:T(8,128)}, f32[64,384]{1,0:T(8,128)S(1)}, u32[]{:S(2)}) copy-start(f32[64,384]{1,0:T(8,128)S(1)} %reshape.237) | copy-start | bytes 294916
  200.1 60.6 %reduce-scatter.15.cloned.1.call-start = ((), (), s32[]{:S(2)}) async-start(), calls=%async_computation.16 | async-start | bytes 245760 | tf_op jit(solution)/shard_map/while/body/eval_jaxpr/reduce_scatter | solution.py:173
  219.0 12.5 %copy-start.22 = (bf16[1,64,1536]{2,1,0:T(8,128)(2,1)S(1)}, bf16[1,64,1536]{2,1,0:T(8,128)(2,1)}, u32[]{:S(2)}) copy-start(bf16[1,64,1536]{2,1,0:T(8,128)(2,1)} %all-gather) | copy-start | bytes 589828
  220.0 42.3 %copy-start.36 = (f32[16]{0:T(128)}, f32[16]{0:T(128)S(1)}, u32[]{:S(2)}) copy-start(f32[16]{0:T(128)S(1)} %broadcast_multiply_fusion.7) | copy-start | bytes 196
  221.0 41.2 %copy-start.41 = (f32[16]{0:T(128)}, f32[16]{0:T(128)S(1)}, u32[]{:S(2)}) copy-start(f32[16]{0:T(128)S(1)} %add_rsqrt_fusion.1) | copy-start | bytes 196
  236.2 24.5 %copy-start.17 = (bf16[16,1536]{1,0:T(8,128)(2,1)S(1)}, bf16[16,1536]{1,0:T(8,128)(2,1)}, u32[]{:S(2)}) copy-start(bf16[16,1536]{1,0:T(8,128)(2,1)} %reduce-scatter.11.cloned.1.call-done) | copy-start | bytes 147460
  236.2 26.1 %copy-start.25 = (bf16[1,16,1536]{2,1,0:T(8,128)(2,1)S(1)}, bf16[1,16,1536]{2,1,0:T(8,128)(2,1)}, u32[]{:S(2)}) copy-start(bf16[1,16,1536]{2,1,0:T(8,128)(2,1)} %param.33) | copy-start | bytes 147460
  240.8 54.6 %copy-start.55 = (pred[2112]{0:T(1024)(128)(4,1)S(1)}, pred[2112]{0:T(1024)(128)(4,1)}, u32[]{:S(2)}) copy-start(pred[2112]{0:T(1024)(128)(4,1)} %copy-done.54) | copy-start | bytes 6340
  240.8 152.7 %all-gather.16.cloned.1.call-start = ((), (), s32[]{:S(2)}) async-start(), calls=%async_computation.17 | async-start | bytes 11796480 | tf_op jit(solution)/shard_map/all_gather | solution.py:83
  241.5 188.5 %reduce-scatter.19.cloned.1.call-start = ((), (), s32[]{:S(2)}) async-start(), calls=%async_computation.20 | async-start | bytes 1327104 | tf_op jit(solution)/shard_map/reduce_scatter | solution.py:315
  262.2 37.3 %copy-start.50 = (f32[16]{0:T(128)}, f32[16]{0:T(128)S(1)}, u32[]{:S(2)}) copy-start(f32[16]{0:T(128)S(1)} %get-tuple-element.159) | copy-start | bytes 196
  262.2 37.3 %copy-start.52 = (f32[16]{0:T(128)}, f32[16]{0:T(128)S(1)}, u32[]{:S(2)}) copy-start(f32[16]{0:T(128)S(1)} %get-tuple-element.160) | copy-start | bytes 196
  271.9 191.0 %reduce-scatter.17.cloned.1.call-start = ((), (), s32[]{:S(2)}) async-start(), calls=%async_computation.19 | async-start | bytes 1327104 | tf_op jit(solution)/shard_map/reduce_scatter | solution.py:306
  311.9 262.1 %all-reduce.11.cloned.1.call-start = ((), (), s32[]{:S(2)}) async-start(), calls=%async_computation.24 | async-start | bytes 4718592
  316.8 11.0 %copy-start.4 = (bf16[4,96,2112]{2,1,0:T(8,128)(2,1)}, bf16[4,96,2112]{2,1,0:T(8,128)(2,1)S(1)}, u32[]{:S(2)}) copy-start(bf16[4,96,2112]{2,1,0:T(8,128)(2,1)S(1)} %convolution_convert_fusion.3) | copy-start | bytes 4866052
  334.6 277.5 %all-gather.18.cloned.1.call-start = ((), (), s32[]{:S(2)}) async-start(), calls=%async_computation.18 | async-start | bytes 5898240 | tf_op jit(solution)/shard_map/all_gather | solution.py:82
  347.6 41.7 %all-to-all-start = ((bf16[2048,2,384]{2,1,0:T(2,128)(2,1)}), bf16[2048,2,384]{2,1,0:T(2,128)(2,1)}, u32[]{:S(2)}, u32[]{:S(2)}) async-start(bf16[2048,2,384]{2,1,0:T(2,128)(2,1)} %copy.126), calls=%async_computation.3 | async-start | bytes 6291456 | tf_op jit(solution)/shard_map/while/body/eval_jaxpr/all_to_all | solution.py:230
  352.3 307.3 %reduce-scatter.13.cloned.1.call-start = ((), (), s32[]{:S(2)}) async-start(), calls=%async_computation.15 | async-start | bytes 245760 | tf_op jit(solution)/shard_map/while/body/eval_jaxpr/reduce_scatter | solution.py:158
  357.0 378.5 %reduce-scatter.25.cloned.1.call-start = ((), (), s32[]{:S(2)}) async-start(), calls=%async_computation.23 | async-start | bytes 811008
  409.3 424.6 %reduce-scatter.21.cloned.1.call-start = ((), (), s32[]{:S(2)}) async-start(), calls=%async_computation.21 | async-start | bytes 5308416 | tf_op jit(solution)/shard_map/reduce_scatter | solution.py:300
  412.9 519.8 %reduce-scatter.23.cloned.1.call-start = ((), (), s32[]{:S(2)}) async-start(), calls=%async_computation.22 | async-start | bytes 5308416 | tf_op jit(solution)/shard_map/reduce_scatter | solution.py:303
  417.8 7.1 copy-start.56
  421.3 8.6 all-to-all-start.1
  576.0 36.2 %copy-start.40 = (f32[16]{0:T(128)S(1)}, f32[16]{0:T(128)}, u32[]{:S(2)}) copy-start(f32[16]{0:T(128)} %copy-done.39) | copy-start | bytes 196
  576.0 36.2 %copy-start.49 = (f32[16]{0:T(128)S(1)}, f32[16]{0:T(128)}, u32[]{:S(2)}) copy-start(f32[16]{0:T(128)} %copy-done.48) | copy-start | bytes 196
  582.2 33.7 %copy-start.31 = (f32[1536]{0:T(1024)S(1)}, f32[1536]{0:T(1024)}, u32[]{:S(2)}) copy-start(f32[1536]{0:T(1024)} %get-tuple-element.98) | copy-start | bytes 18436
  582.2 33.8 %copy-start.46 = (f32[1536]{0:T(1024)S(1)}, f32[1536]{0:T(1024)}, u32[]{:S(2)}) copy-start(f32[1536]{0:T(1024)} %get-tuple-element.87) | copy-start | bytes 18436
  582.2 33.8 %copy-start.47 = (f32[1536]{0:T(1024)S(1)}, f32[1536]{0:T(1024)}, u32[]{:S(2)}) copy-start(f32[1536]{0:T(1024)} %get-tuple-element.90) | copy-start | bytes 18436
  582.2 77.3 %copy-start.24 = (bf16[16,1536]{1,0:T(8,128)(2,1)S(1)}, bf16[16,1536]{1,0:T(8,128)(2,1)}, u32[]{:S(2)}) copy-start(bf16[16,1536]{1,0:T(8,128)(2,1)} %reduce-scatter.15.cloned.1.call-done) | copy-start | bytes 147460
  582.2 77.3 %copy-start.26 = (bf16[1,16,1536]{2,1,0:T(8,128)(2,1)S(1)}, bf16[1,16,1536]{2,1,0:T(8,128)(2,1)}, u32[]{:S(2)}) copy-start(bf16[1,16,1536]{2,1,0:T(8,128)(2,1)} %param.33) | copy-start | bytes 147460
  582.3 77.3 %copy-start.37 = (f32[16]{0:T(128)S(1)}, f32[16]{0:T(128)}, u32[]{:S(2)}) copy-start(f32[16]{0:T(128)} %copy-done.36) | copy-start | bytes 196
  582.3 77.3 %copy-start.42 = (f32[16]{0:T(128)S(1)}, f32[16]{0:T(128)}, u32[]{:S(2)}) copy-start(f32[16]{0:T(128)} %copy-done.41) | copy-start | bytes 196
  582.3 77.3 %copy-start.51 = (f32[16]{0:T(128)S(1)}, f32[16]{0:T(128)}, u32[]{:S(2)}) copy-start(f32[16]{0:T(128)} %copy-done.50) | copy-start | bytes 196
  582.3 77.3 %copy-start.53 = (f32[16]{0:T(128)S(1)}, f32[16]{0:T(128)}, u32[]{:S(2)}) copy-start(f32[16]{0:T(128)} %copy-done.52) | copy-start | bytes 196
  612.1 322.7 %copy-start.1 = (bf16[8,1536]{1,0:T(8,128)(2,1)S(1)}, bf16[8,1536]{1,0:T(8,128)(2,1)}, u32[]{:S(2)}) copy-start(bf16[8,1536]{1,0:T(8,128)(2,1)} %param.21) | copy-start | bytes 73732
  (28 other events, 75.4 us)
Sparse Core Ops, SparseCore 0:
  10.2 43.8 all-gather.11
  56.8 50.4 all-gather.9
  109.5 44.8 all-gather.7
  156.5 41.1 all-gather.13
  200.5 18.4 reduce-scatter.10
  240.9 19.7 reduce-scatter.14
  262.3 64.0 all-gather.15
  330.4 64.8 reduce-scatter.18
  399.2 63.7 reduce-scatter.16
  466.4 107.5 all-reduce.10
  575.6 36.5 all-gather.17
  614.4 19.8 reduce-scatter.12
  639.4 96.1 reduce-scatter.24
  739.1 94.7 reduce-scatter.20
  837.3 95.2 reduce-scatter.22
where the time goes:
time: 944 us; the launch traced here: 941 us
  waiting for transfers between devices  649 us (69%)
  matrix products  95.8 us (10%)
  blocking collectives  87.2 us (9%)
  local copies, waits for them, and re-layouts  54.7 us (6%)
  other arithmetic  28.2 us (3%)
  between operations  17.4 us (2%)
    unnamed x17, waiting for transfers between devices  187 us
    reduce_scatter x1, waiting for transfers between devices, body(): lax.psum_scatter(up_acc.astype(jnp.bfloat16), 'wide', scatter_dimension=0...  96.9 us
    reduce_scatter x1, waiting for transfers between devices, body(): lax.psum_scatter(down_acc.astype(jnp.bfloat16), 'wide', scatter_dimension...  96.6 us
    all_gather x1, waiting for transfers between devices, body(): lax.all_gather(keyval_weight, 'wide', axis=0, tiled=True)  51.6 us
    all_gather x1, waiting for transfers between devices, item_step(): lax.all_gather(media_nf.astype(jnp.bfloat16), 'narrow', axis=0, tiled=True)  42.8 us
    unnamed x1, blocking collectives  40.1 us
    all_to_all x1, waiting for transfers between devices, item_step(): lax.all_to_all(media_pairs, 'narrow', split_axis=0, concat_axis=2, tiled=...  31.9 us
    reduce_scatter x1, waiting for transfers between devices, body(): lax.psum_scatter(query_acc.astype(jnp.bfloat16), 'wide', scatter_dimensio...  31.3 us
  transfers between devices with their start and end apart: 17, of which 14 were waited for; matrix products, arithmetic and copies ran while one was open for 16% of the time, Pallas kernels for 0%

commit v1 on v0

--- a/solution.py
+++ b/solution.py
@@ -1,3 +1,4 @@
+import functools
 import math
 import jax
 import jax.numpy as jnp
@@ -11,6 +12,26 @@
 EPS = 1e-05
 ENT_COEF = 4.0
 HIGH = lax.Precision.HIGHEST
+
+
+def _use_orders(xin, ax_name, dimension_no):
+    m_next, r2, v_next = (lax.axis_size(ax_name), lax.axis_index(ax_name), xin.shape[dimension_no])
+    val, inter = (xin, 1)
+    while inter < m_next:
+        val = jnp.concatenate(
+            [
+                val,
+                lax.ppermute(
+                    val, ax_name, perm=[(pp, (pp - inter) % m_next) for pp in range(m_next)]
+                ),
+            ],
+            axis=dimension_no,
+        )
+        inter = 2 * inter
+    return jnp.roll(val, shift=r2 * v_next, axis=dimension_no)
+
+
+sheet_time = functools.partial(_use_orders, ax_name="narrow", dimension_no=1)
 
 
 def norm_forward(values, norm_gain, norm_bias):
@@ -79,7 +100,7 @@
         lax.all_gather(output_weight, "wide", axis=1, tiled=True),
     )
     query_full, keyval_full = (
-        lax.all_gather(query_own, "narrow", axis=1, tiled=True),
+        sheet_time(query_own),
         lax.all_gather(keyval_own, "narrow", axis=2, tiled=True),
     )
     keyval_flat = keyval_own.reshape(width, 2 * cols)

time: 944 us -> 913 us (0.967)
  waiting for transfers between devices: 649 us -> 593 us
  local copies, waits for them, and re-layouts: 54.7 us -> 67.1 us
    ppermute x0 -> x2, waiting for transfers between devices: none -> 62.8 us  [_use_orders(): lax.ppermute(val, ax_name, perm=[(pp, (pp - inter) % m_next) for pp in ra...]
    unnamed x17 -> x16, waiting for transfers between devices: 187 us -> 131 us
    reduce_scatter x1, waiting for transfers between devices: 31.3 us -> 0.01 us  [body(): lax.psum_scatter(query_acc.astype(jnp.bfloat16), 'wide', scatter_dimensio...]
    all_gather x1 -> x0, waiting for transfers between devices: 29.8 us -> none  [body(): lax.all_gather(query_own, 'narrow', axis=1, tiled=True)]
    unnamed x128 -> x139, local copies, waits for them, and re-layouts: 15.5 us -> 23.7 us
  transfers between devices with their start and end apart: 17 -> 18, of which waited for: 14 -> 14; matrix products, arithmetic and copies ran while one was open for 16% -> 19% of each run, Pallas kernels for 0% -> 0%
where the time goes in v1:
time: 913 us; the launch traced here: 902 us
  waiting for transfers between devices  593 us (65%)
  matrix products  96.4 us (11%)
  blocking collectives  87.4 us (10%)
  local copies, waits for them, and re-layouts  67.1 us (7%)
  other arithmetic  30.8 us (3%)
  between operations  17.5 us (2%)
  starting transfers between devices  10.5 us (1%)
    unnamed x16, waiting for transfers between devices  131 us
    reduce_scatter x1, waiting for transfers between devices, body(): lax.psum_scatter(down_acc.astype(jnp.bfloat16), 'wide', scatter_dimension...  97 us
    reduce_scatter x1, waiting for transfers between devices, body(): lax.psum_scatter(up_acc.astype(jnp.bfloat16), 'wide', scatter_dimension=0...  96.6 us
    ppermute x2, waiting for transfers between devices, _use_orders(): lax.ppermute(val, ax_name, perm=[(pp, (pp - inter) % m_next) for pp in ra...  62.8 us
    all_gather x1, waiting for transfers between devices, body(): lax.all_gather(keyval_weight, 'wide', axis=0, tiled=True)  51.6 us
    all_gather x1, waiting for transfers between devices, item_step(): lax.all_gather(media_nf.astype(jnp.bfloat16), 'narrow', axis=0, tiled=True)  42.7 us
    unnamed x1, blocking collectives  40.3 us
    all_to_all x1, waiting for transfers between devices, item_step(): lax.all_to_all(media_pairs, 'narrow', split_axis=0, concat_axis=2, tiled=...  31.7 us
  transfers between devices with their start and end apart: 18, of which 14 were waited for; matrix products, arithmetic and copies ran while one was open for 19% of the time, Pallas kernels for 0%

profile of v1, /device:TPU:0, one launch (start us, length us, event | category | flops | bytes accessed | tf_op | source)
XLA Modules:
  0.0 902.5 jit_solution(5582456053386781968)
XLA Ops:
  16.0 6.9 all_gather.33
  23.5 30.5 %all-gather.11.cloned.1.call-done = bf16[1536,384]{1,0:T(8,128)(2,1)} async-done(((bf16[192,384]{1,0:T(8,128)(2,1)}), bf16[1536,384]{1,0:T(8,128)(2,1)}) %all-gather.11.cloned.1.call-update) | async-done | bytes 1179664 | tf_op jit(solution)/shard_map/all_gather | solution.py:98
  55.8 51.6 %all-gather.9.cloned.1.call-done = bf16[1536,2,384]{2,0,1:T(8,128)(2,1)} async-done(((bf16[192,2,384]{2,0,1:T(8,128)(2,1)}), bf16[1536,2,384]{2,0,1:T(8,128)(2,1)}) %all-gather.9.cloned.1.call-update) | async-done | bytes 2359312 | tf_op jit(solution)/shard_map/all_gather | solution.py:99
  107.4 4.3 copy.117
  111.7 42.7 %all-gather.7.cloned.1.call-done = bf16[2048,1536]{1,0:T(8,128)(2,1)} async-done(((bf16[512,1536]{1,0:T(8,128)(2,1)}), bf16[2048,1536]{1,0:T(8,128)(2,1)}) %all-gather.7.cloned.1.call-update) | async-done | bytes 6291472 | tf_op jit(solution)/shard_map/while/body/eval_jaxpr/all_gather | solution.py:136
  154.4 3.3 constant_dynamic-update-slice_fusion.1
  157.9 5.5 convolution_convert_fusion.2
  165.4 3.8 copy.119
  169.2 3.8 copy.118
  173.0 3.6 fusion.88
  176.6 3.0 convolution_bitcast_fusion.3
  181.4 16.5 %all-gather.13.cloned.1.call-done = bf16[384,1536]{0,1:T(8,128)(2,1)} async-done(((bf16[384,192]{0,1:T(8,128)(2,1)}), bf16[384,1536]{0,1:T(8,128)(2,1)}) %all-gather.13.cloned.1.call-update) | async-done | bytes 1179664 | tf_op jit(solution)/shard_map/all_gather | solution.py:100
  200.4 6.9 all-gather
  207.2 11.7 %reduce-scatter.11.cloned.1.call-done = bf16[16,1536]{1,0:T(8,128)(2,1)} async-done(((bf16[64,1536]{1,0:T(8,128)(2,1)}), bf16[16,1536]{1,0:T(8,128)(2,1)}) %reduce-scatter.11.cloned.1.call-update) | async-done | bytes 49168 | tf_op jit(solution)/shard_map/while/body/eval_jaxpr/reduce_scatter | solution.py:167
  221.9 5.6 all_gather.37
  228.2 3.3 fusion.91
  231.5 4.0 fusion.10
  236.2 4.6 convolution_convert_fusion.7
  241.6 19.1 %reduce-scatter.15.cloned.1.call-done = bf16[16,1536]{1,0:T(8,128)(2,1)} async-done(((bf16[64,1536]{1,0:T(8,128)(2,1)}), bf16[16,1536]{1,0:T(8,128)(2,1)}) %reduce-scatter.15.cloned.1.call-update) | async-done | bytes 49168 | tf_op jit(solution)/shard_map/while/body/eval_jaxpr/reduce_scatter | solution.py:194
  263.2 5.6 all_gather.39
  269.4 2.5 convolution_convert_fusion.5
  272.7 22.1 %psum.7 = f32[]{:T(128)} all-reduce(f32[]{:T(128)S(6)} %add.206), channel_id=1, replica_groups=mesh['wide'=8,'narrow'=4] {'wide'}, use_global_device_ids=true, to_apply=%region_14.15 | all-reduce | flops 1 | bytes 8 | tf_op jit(solution)/shard_map/psum | solution.py:94
  295.5 4.2 multiply_reduce_fusion.4
  305.6 3.6 fusion.8
  315.4 2.9 convolution_convert_fusion.3
  318.3 10.9 %convolution_convert_fusion.4 = bf16[1536,768]{0,1:T(8,128)(2,1)} fusion(bf16[2112,1536]{1,0:T(8,128)(2,1)} %copy-done.9, bf16[2112,384]{0,1:T(8,128)(2,1)S(1)} %bitcast.159, bf16[2112,384]{0,1:T(8,128)(2,1)S(1)} %bitcast.154), kind=kOutput, calls=%fused_computation.21 | convolution fusion | flops 4990500864 | bytes 12091392 | tf_op jit(solution)/shard_map/while/body/eval_jaxpr/kd,ke->de/dot_general | solution.py:236
  329.2 6.9 copy.135
  336.1 3.6 fusion.9
  339.7 8.7 copy.126
  348.4 4.8 all-to-all-start
  353.2 4.7 convolution_convert_fusion.8
  358.5 31.7 %all-to-all-done = bf16[2048,2,384]{2,1,0:T(2,128)(2,1)} async-done(((bf16[2048,2,384]{2,1,0:T(2,128)(2,1)}), bf16[2048,2,384]{2,1,0:T(2,128)(2,1)}, u32[]{:S(2)}, u32[]{:S(2)}) %all-to-all-start) | async-done | bytes 3145760 | tf_op jit(solution)/shard_map/while/body/eval_jaxpr/all_to_all | solution.py:251
  394.5 9.9 %multiply_reduce_fusion = (f32[1536]{0:T(1024)}, f32[512]{0:T(512)S(1)}, f32[512]{0:T(512)S(1)}, f32[1536]{0:T(1024)}, f32[512,1536]{1,0:T(8,128)S(1)}) fusion(f32[512,1536]{1,0:T(8,128)S(1)} %get-tuple-element.150, f32[512]{0:T(512)S(1)} %add_rsqrt_fusion, f32[512]{0:T(512)S(1)} %broadcast_multiply_fusion.2, f32[1536]{0:T(1024)S(1)} %copy-done.36, ...), kind=kOutput, calls=%fused_computation.25 | convolution fusion | flops 4838912000 | bytes 18900992 | tf_op jit(solution)/shard_map/while/body/eval_jaxpr/rsc,dsc->rd/dot_general | solution.py:254
  406.5 3.6 convolution_bitcast_fusion.1
  410.2 3.9 convolution_convert_fusion
  415.2 3.6 convolution_convert_fusion.1
  420.1 13.7 %collective-permute-done = bf16[1536,384]{1,0:T(8,128)(2,1)S(1)} collective-permute-done((bf16[1536,384]{1,0:T(8,128)(2,1)S(1)}, bf16[1536,384]{1,0:T(8,128)(2,1)S(1)}, u32[]{:S(2)}, u32[]{:S(2)}) %collective-permute-start) | collective-permute-done | bytes 1179680 | tf_op jit(solution)/shard_map/ppermute | solution.py:24
  440.5 49.1 %collective-permute-done.1 = bf16[1536,768]{1,0:T(8,128)(2,1)} collective-permute-done((bf16[1536,768]{1,0:T(8,128)(2,1)}, bf16[1536,768]{1,0:T(8,128)(2,1)}, u32[]{:S(2)}, u32[]{:S(2)}) %collective-permute-start.1) | collective-permute-done | bytes 2359328 | tf_op jit(solution)/shard_map/ppermute | solution.py:24
  489.6 3.3 constant_dynamic-update-slice_fusion.5
  497.5 3.5 all-to-all-start.1
  501.1 3.3 constant_dynamic-update-slice_fusion.2
  509.7 63.9 %all-reduce.11.cloned.1.call-done = bf16[1536,2,384]{2,1,0:T(2,128)(2,1)} async-done(((bf16[1536,2,384]{2,1,0:T(2,128)(2,1)}), bf16[1536,2,384]{2,1,0:T(2,128)(2,1)}) %all-reduce.11.cloned.1.call-update) | async-done | bytes 2359312
  575.5 6.2 convolution_bitcast_fusion.2
  581.9 4.4 fusion.58
  586.3 40.3 %all-reduce.8 = (f32[1536]{0:T(1024)S(1)}, f32[1536]{0:T(1024)S(1)}, f32[1536]{0:T(1024)S(1)}, f32[1536]{0:T(1024)S(1)}, f32[1536]{0:T(1024)S(1)}, /*index=5*/f32[1536]{0:T(1024)S(1)}) all-reduce(f32[1536]{0:T(1024)S(1)} %copy-done.49, f32[1536]{0:T(1024)S(1)} %copy-done.50, ...), channel_id=7, replica_groups=mesh['wide'=8,'narrow'=4] {'wide','narrow'}, use_global_device_ids=true, to_apply=%region_23.24.clone | all-reduce | flops 9216 | bytes 73728
  631.7 64.6 %reduce-scatter.25.cloned.1.call-done = f32[48,8]{1,0:T(8,128)} async-done(((f32[1536,8]{1,0:T(8,128)}), f32[48,8]{1,0:T(8,128)}) %reduce-scatter.25.cloned.1.call-update) | async-done | bytes 1552
  697.8 97.0 %reduce-scatter.23.cloned.1.call-done = bf16[1536,192]{0,1:T(8,128)(2,1)} async-done(((bf16[1536,1536]{0,1:T(8,128)(2,1)}), bf16[1536,192]{0,1:T(8,128)(2,1)}) %reduce-scatter.23.cloned.1.call-update) | async-done | bytes 589840 | tf_op jit(solution)/shard_map/reduce_scatter | solution.py:324
  796.9 96.6 %reduce-scatter.21.cloned.1.call-done = bf16[192,1536]{1,0:T(8,128)(2,1)} async-done(((bf16[1536,1536]{1,0:T(8,128)(2,1)}), bf16[192,1536]{1,0:T(8,128)(2,1)}) %reduce-scatter.21.cloned.1.call-update) | async-done | bytes 589840 | tf_op jit(solution)/shard_map/reduce_scatter | solution.py:321
  (232 shorter events, 75.1 us)
Async XLA Ops:
  7.2 46.9 %all-gather.11.cloned.1.call-start = ((), (), s32[]{:S(2)}) async-start(), calls=%async_computation.12 | async-start | bytes 1327104 | tf_op jit(solution)/shard_map/all_gather | solution.py:98
  7.9 99.4 %all-gather.9.cloned.1.call-start = ((), (), s32[]{:S(2)}) async-start(), calls=%async_computation.11 | async-start | bytes 2654208 | tf_op jit(solution)/shard_map/all_gather | solution.py:99
  9.7 144.7 %all-gather.7.cloned.1.call-start = ((), (), s32[]{:S(2)}) async-start(), calls=%async_computation.10 | async-start | bytes 7864320 | tf_op jit(solution)/shard_map/while/body/eval_jaxpr/all_gather | solution.py:136
  12.5 10.4 %copy-start.48 = (s32[1,2048]{1,0:T(1,128)S(1)}, s32[1,2048]{1,0:T(1,128)}, u32[]{:S(2)}) copy-start(s32[1,2048]{1,0:T(1,128)} %param.20) | copy-start | bytes 24580
  14.2 183.6 %all-gather.13.cloned.1.call-start = ((), (), s32[]{:S(2)}) async-start(), calls=%async_computation.13 | async-start | bytes 1327104 | tf_op jit(solution)/shard_map/all_gather | solution.py:100
  14.8 204.2 %reduce-scatter.11.cloned.1.call-start = ((), (), s32[]{:S(2)}) async-start(), calls=%async_computation.14 | async-start | bytes 245760 | tf_op jit(solution)/shard_map/while/body/eval_jaxpr/reduce_scatter | solution.py:167
  15.6 7.2 copy-start.42
  15.9 7.0 copy-start.51
  23.5 149.5 %copy-start.57 = (pred[2112]{0:T(1024)(128)(4,1)}, pred[2112]{0:T(1024)(128)(4,1)S(1)}, u32[]{:S(2)}) copy-start(pred[2112]{0:T(1024)(128)(4,1)S(1)} %concatenate.28) | copy-start | bytes 6340
  55.8 117.2 %copy-start.30 = (bf16[64,4,96]{2,1,0:T(4,128)(2,1)}, bf16[64,4,96]{2,1,0:T(4,128)(2,1)S(1)}, u32[]{:S(2)}) copy-start(bf16[64,4,96]{2,1,0:T(4,128)(2,1)S(1)} %reshape.235) | copy-start | bytes 147460
  157.8 5.6 copy-start.9
  176.6 129.0 %copy-start.60 = (f32[4,64]{1,0:T(4,128)}, f32[4,64]{1,0:T(4,128)S(1)}, u32[]{:S(2)}) copy-start(f32[4,64]{1,0:T(4,128)S(1)} %get-tuple-element.151) | copy-start | bytes 3076
  176.6 44.3 %copy-start.31 = (f32[1536]{0:T(1024)S(1)}, f32[1536]{0:T(1024)}, u32[]{:S(2)}) copy-start(f32[1536]{0:T(1024)} %param.26) | copy-start | bytes 18436
  176.6 44.4 %copy-start.47 = (f32[1536]{0:T(1024)S(1)}, f32[1536]{0:T(1024)}, u32[]{:S(2)}) copy-start(f32[1536]{0:T(1024)} %param.27) | copy-start | bytes 18436
  181.4 50.1 %copy-start.21 = (f32[64,384]{1,0:T(8,128)}, f32[64,384]{1,0:T(8,128)S(1)}, u32[]{:S(2)}) copy-start(f32[64,384]{1,0:T(8,128)S(1)} %reshape.237) | copy-start | bytes 294916
  200.3 60.4 %reduce-scatter.15.cloned.1.call-start = ((), (), s32[]{:S(2)}) async-start(), calls=%async_computation.16 | async-start | bytes 245760 | tf_op jit(solution)/shard_map/while/body/eval_jaxpr/reduce_scatter | solution.py:194
  219.0 12.5 %copy-start.25 = (bf16[1,64,1536]{2,1,0:T(8,128)(2,1)S(1)}, bf16[1,64,1536]{2,1,0:T(8,128)(2,1)}, u32[]{:S(2)}) copy-start(bf16[1,64,1536]{2,1,0:T(8,128)(2,1)} %all-gather) | copy-start | bytes 589828
  220.0 42.3 %copy-start.39 = (f32[16]{0:T(128)}, f32[16]{0:T(128)S(1)}, u32[]{:S(2)}) copy-start(f32[16]{0:T(128)S(1)} %broadcast_multiply_fusion.7) | copy-start | bytes 196
  221.0 41.2 %copy-start.44 = (f32[16]{0:T(128)}, f32[16]{0:T(128)S(1)}, u32[]{:S(2)}) copy-start(f32[16]{0:T(128)S(1)} %add_rsqrt_fusion.1) | copy-start | bytes 196
  236.2 24.5 %copy-start.20 = (bf16[16,1536]{1,0:T(8,128)(2,1)S(1)}, bf16[16,1536]{1,0:T(8,128)(2,1)}, u32[]{:S(2)}) copy-start(bf16[16,1536]{1,0:T(8,128)(2,1)} %reduce-scatter.11.cloned.1.call-done) | copy-start | bytes 147460
  236.2 26.0 %copy-start.28 = (bf16[1,16,1536]{2,1,0:T(8,128)(2,1)S(1)}, bf16[1,16,1536]{2,1,0:T(8,128)(2,1)}, u32[]{:S(2)}) copy-start(bf16[1,16,1536]{2,1,0:T(8,128)(2,1)} %param.33) | copy-start | bytes 147460
  240.7 54.8 %copy-start.58 = (pred[2112]{0:T(1024)(128)(4,1)S(1)}, pred[2112]{0:T(1024)(128)(4,1)}, u32[]{:S(2)}) copy-start(pred[2112]{0:T(1024)(128)(4,1)} %copy-done.57) | copy-start | bytes 6340
  240.8 153.7 %all-gather.15.cloned.1.call-start = ((), (), s32[]{:S(2)}) async-start(), calls=%async_computation.17 | async-start | bytes 11796480 | tf_op jit(solution)/shard_map/all_gather | solution.py:104
  241.5 264.9 %reduce-scatter.19.cloned.1.call-start = ((), (), s32[]{:S(2)}) async-start(), calls=%async_computation.19 | async-start | bytes 1327104 | tf_op jit(solution)/shard_map/reduce_scatter | solution.py:336
  262.2 37.5 %copy-start.53 = (f32[16]{0:T(128)}, f32[16]{0:T(128)S(1)}, u32[]{:S(2)}) copy-start(f32[16]{0:T(128)S(1)} %get-tuple-element.159) | copy-start | bytes 196
  262.2 37.5 %copy-start.55 = (f32[16]{0:T(128)}, f32[16]{0:T(128)S(1)}, u32[]{:S(2)}) copy-start(f32[16]{0:T(128)S(1)} %get-tuple-element.160) | copy-start | bytes 196
  272.0 236.1 %reduce-scatter.17.cloned.1.call-start = ((), (), s32[]{:S(2)}) async-start(), calls=%async_computation.18 | async-start | bytes 1327104 | tf_op jit(solution)/shard_map/reduce_scatter | solution.py:327
  313.4 260.2 %all-reduce.11.cloned.1.call-start = ((), (), s32[]{:S(2)}) async-start(), calls=%async_computation.23 | async-start | bytes 4718592
  318.3 10.9 %copy-start.7 = (bf16[4,96,2112]{2,1,0:T(8,128)(2,1)}, bf16[4,96,2112]{2,1,0:T(8,128)(2,1)S(1)}, u32[]{:S(2)}) copy-start(bf16[4,96,2112]{2,1,0:T(8,128)(2,1)S(1)} %convolution_convert_fusion.3) | copy-start | bytes 4866052
  348.4 41.7 %all-to-all-start = ((bf16[2048,2,384]{2,1,0:T(2,128)(2,1)}), bf16[2048,2,384]{2,1,0:T(2,128)(2,1)}, u32[]{:S(2)}, u32[]{:S(2)}) async-start(bf16[2048,2,384]{2,1,0:T(2,128)(2,1)} %copy.126), calls=%async_computation.3 | async-start | bytes 6291456 | tf_op jit(solution)/shard_map/while/body/eval_jaxpr/all_to_all | solution.py:251
  353.2 276.9 %reduce-scatter.13.cloned.1.call-start = ((), (), s32[]{:S(2)}) async-start(), calls=%async_computation.15 | async-start | bytes 245760 | tf_op jit(solution)/shard_map/while/body/eval_jaxpr/reduce_scatter | solution.py:179
  357.9 338.4 %reduce-scatter.25.cloned.1.call-start = ((), (), s32[]{:S(2)}) async-start(), calls=%async_computation.22 | async-start | bytes 811008
  410.2 384.5 %reduce-scatter.23.cloned.1.call-start = ((), (), s32[]{:S(2)}) async-start(), calls=%async_computation.21 | async-start | bytes 5308416 | tf_op jit(solution)/shard_map/reduce_scatter | solution.py:324
  414.2 479.4 %reduce-scatter.21.cloned.1.call-start = ((), (), s32[]{:S(2)}) async-start(), calls=%async_computation.20 | async-start | bytes 5308416 | tf_op jit(solution)/shard_map/reduce_scatter | solution.py:321
  420.1 16.7 %copy-start.59 = (u32[32]{0:T(128)S(1)}, u32[32]{0:T(128)}, u32[]{:S(2)}) copy-start(u32[32]{0:T(128)} %constant.242) | copy-start | bytes 388
  420.1 13.7 %collective-permute-start = (bf16[1536,384]{1,0:T(8,128)(2,1)S(1)}, bf16[1536,384]{1,0:T(8,128)(2,1)S(1)}, u32[]{:S(2)}, u32[]{:S(2)}) collective-permute-start(bf16[1536,384]{1,0:T(8,128)(2,1)S(1)} %copy-done.2), channel_id=1, source_target_pairs={{0,3},{1,0},{2,1},{3,2},{4,7},{5,4},{6,5},{7,6},{8,11},{9,8},{10,9... | collective-permute-start | bytes 3538952 | tf_op jit(solution)/shard_map/ppermute | solution.py:24
  435.6 54.0 %collective-permute-start.1 = (bf16[1536,768]{1,0:T(8,128)(2,1)}, bf16[1536,768]{1,0:T(8,128)(2,1)}, u32[]{:S(2)}, u32[]{:S(2)}) collective-permute-start(bf16[1536,768]{1,0:T(8,128)(2,1)} %pad_maximum_fusion.2), channel_id=1, source_target_pairs={{0,2},{1,3},{2,0},{3,1},{4,6},{5,7},{6,4},{7,5},{8,10},{9,11},{10,... | collective-permute-start | bytes 7077896 | tf_op jit(solution)/shard_map/ppermute | solution.py:24
  440.5 53.6 %copy-start.6 = (bf16[1536,384]{1,0:T(8,128)(2,1)S(1)}, bf16[1536,384]{1,0:T(8,128)(2,1)}, u32[]{:S(2)}) copy-start(bf16[1536,384]{1,0:T(8,128)(2,1)} %copy-done.5) | copy-start | bytes 3538948
  497.5 8.8 all-to-all-start.1
  575.5 6.2 copy-start.43
  575.5 6.2 copy-start.52
  581.8 48.3 %copy-start.27 = (bf16[16,1536]{1,0:T(8,128)(2,1)S(1)}, bf16[16,1536]{1,0:T(8,128)(2,1)}, u32[]{:S(2)}) copy-start(bf16[16,1536]{1,0:T(8,128)(2,1)} %reduce-scatter.15.cloned.1.call-done) | copy-start | bytes 147460
  581.8 48.3 %copy-start.29 = (bf16[1,16,1536]{2,1,0:T(8,128)(2,1)S(1)}, bf16[1,16,1536]{2,1,0:T(8,128)(2,1)}, u32[]{:S(2)}) copy-start(bf16[1,16,1536]{2,1,0:T(8,128)(2,1)} %param.33) | copy-start | bytes 147460
  581.8 48.3 %copy-start.40 = (f32[16]{0:T(128)S(1)}, f32[16]{0:T(128)}, u32[]{:S(2)}) copy-start(f32[16]{0:T(128)} %copy-done.39) | copy-start | bytes 196
  581.8 48.3 %copy-start.45 = (f32[16]{0:T(128)S(1)}, f32[16]{0:T(128)}, u32[]{:S(2)}) copy-start(f32[16]{0:T(128)} %copy-done.44) | copy-start | bytes 196
  581.9 48.3 %copy-start.54 = (f32[16]{0:T(128)S(1)}, f32[16]{0:T(128)}, u32[]{:S(2)}) copy-start(f32[16]{0:T(128)} %copy-done.53) | copy-start | bytes 196
  581.9 48.3 %copy-start.56 = (f32[16]{0:T(128)S(1)}, f32[16]{0:T(128)}, u32[]{:S(2)}) copy-start(f32[16]{0:T(128)} %copy-done.55) | copy-start | bytes 196
  581.9 313.9 %copy-start.1 = (bf16[8,1536]{1,0:T(8,128)(2,1)S(1)}, bf16[8,1536]{1,0:T(8,128)(2,1)}, u32[]{:S(2)}) copy-start(bf16[8,1536]{1,0:T(8,128)(2,1)} %param.21) | copy-start | bytes 73732
  (32 other events, 92.9 us)
Sparse Core Ops, SparseCore 0:
  10.2 43.8 all-gather.10
  56.8 50.4 all-gather.8
  109.5 44.8 all-gather.6
  156.5 41.3 all-gather.12
  200.7 18.2 reduce-scatter.10
  240.9 19.7 reduce-scatter.14
  262.3 64.1 all-gather.14
  329.8 64.7 reduce-scatter.18
  398.6 63.7 reduce-scatter.16
  465.8 107.6 all-reduce.10
  576.0 19.0 reduce-scatter.12
  600.0 96.3 reduce-scatter.24
  700.0 94.6 reduce-scatter.22
  798.2 95.2 reduce-scatter.20
